TPU v7x, 256 devices: a whole 4x4x8 slice. The times are simulated.
256 devices in a mesh: group: 16 (over y, x), member: 16 (over z, core).
Axes of the slice: x: 4, y: 4, z: 8, core: 2. Of those that a mesh axis runs over, the one named last changes fastest.
Arguments:
- features: bfloat16 [262144, 1024], P(('group', 'member')), may hold values from -6 to 6
- w_self: bfloat16 [1024, 1024], replicated, may hold values from -0.1875 to 0.1875
- w_neigh: bfloat16 [1024, 1024], replicated, may hold values from -0.1875 to 0.1875
- bias: bfloat16 [1024], replicated, may hold values from -3 to 3
- hub_rows: int32 [1536], P(('group', 'member')), may hold values from 0 to 1023
- hub_nbrs: int32 [262144, 8], P(('group', 'member')), may hold values from 0 to 1535
- local_nbrs: int32 [262144, 16], P(('group', 'member')), may hold values from 0 to 1023
- halo_nbrs: int32 [262144, 16], P(('group', 'member')), may hold values from 0 to 2047
- degrees: int32 [3, 262144], P(None, ('group', 'member')), may hold values from 0 to 16, as said below
- send_rows: int32 [256, 16, 128], P(('group', 'member')), may hold values from 0 to 1023
Outputs:
- hidden_out: bfloat16 [262144, 1024], P(('group', 'member'))
Inputs may be any that keep to these rules, and one draw needn't show every extreme that they name: degrees[0] is at least 1 and reaches 16; degrees[1] reaches 8; degrees[2] reaches 16, each in every draw.
All inputs are finite; a program needn't handle non-finite values.
Results may differ from a plain program's by a relative error of at most 0.002.
Values may be sent and summed in bfloat16 or wider, within the bound.
A program may use at most 128 MiB of HBM per device.

v0:
```python
import math

import jax
import jax.numpy as jnp
from jax import lax
from jax.sharding import PartitionSpec as P


def count_table(index_list, valid_mask, total):
    numbers = jnp.arange(total, dtype=jnp.int32)
    tallies = jnp.zeros((index_list.shape[0], total), jnp.float32)
    for slot in range(index_list.shape[1]):
        hits = (index_list[:, slot][:, None] == numbers[None, :]) & valid_mask[:, slot][:, None]
        tallies = tallies + hits.astype(jnp.float32)
    return tallies.astype(jnp.bfloat16)


def block_mean(
    self_features,
    hub_lookup_matrix,
    neighbour_positions,
    local_index_list,
    hub_index_list,
    halo_index_list,
    deg,
):
    klocal = local_index_list.shape[1]
    khub = hub_index_list.shape[1]
    khalo = halo_index_list.shape[1]
    local_valid_mask = jnp.arange(klocal)[None, :] < deg[0][:, None]
    hub_valid_mask = jnp.arange(khub)[None, :] < deg[1][:, None]
    halo_valid_mask = jnp.arange(khalo)[None, :] < deg[2][:, None]
    local_counts = count_table(local_index_list, local_valid_mask, self_features.shape[0])
    neighbour_sum = jnp.dot(local_counts, self_features, preferred_element_type=jnp.float32)
    hub_counts = count_table(hub_index_list, hub_valid_mask, hub_lookup_matrix.shape[0])
    neighbour_sum = neighbour_sum + jnp.dot(
        hub_counts, hub_lookup_matrix, preferred_element_type=jnp.float32
    )
    halo_counts = count_table(halo_index_list, halo_valid_mask, neighbour_positions.shape[0])
    neighbour_sum = neighbour_sum + jnp.dot(
        halo_counts, neighbour_positions, preferred_element_type=jnp.float32
    )
    count = (
        jnp.sum(local_valid_mask.astype(jnp.float32), axis=1)
        + jnp.sum(hub_valid_mask.astype(jnp.float32), axis=1)
        + jnp.sum(halo_valid_mask.astype(jnp.float32), axis=1)
    )
    return (neighbour_sum / count[:, None]).astype(jnp.bfloat16)


def per_device(
    features, w_self, w_neigh, bias, hub_rows, hub_nbrs, local_nbrs, halo_nbrs, degrees, send_rows
):
    rows_here = features.shape[0]
    width = features.shape[1]
    peers = send_rows.shape[1]
    caps = send_rows.shape[2]
    mine = jnp.take(features, hub_rows, axis=0)
    hub_lookup_matrix = lax.all_gather(mine, ("group", "member"), axis=0, tiled=True)
    outgoing = jnp.take(features, send_rows.reshape(peers * caps), axis=0).reshape(
        peers, caps, width
    )
    received = lax.all_to_all(outgoing, "member", split_axis=0, concat_axis=0, tiled=True)
    neighbour_positions = received.reshape(peers * caps, width)
    blk = math.gcd(rows_here, 256)
    nblocks = rows_here // blk
    local_index_list = local_nbrs.reshape(nblocks, blk, local_nbrs.shape[1])
    hub_index_list = hub_nbrs.reshape(nblocks, blk, hub_nbrs.shape[1])
    halo_index_list = halo_nbrs.reshape(nblocks, blk, halo_nbrs.shape[1])
    deg = degrees.reshape(3, nblocks, blk).transpose(1, 0, 2)

    def one(item):
        return block_mean(
            features, hub_lookup_matrix, neighbour_positions, item[0], item[1], item[2], item[3]
        )

    neigh_mean = lax.map(one, (local_index_list, hub_index_list, halo_index_list, deg)).reshape(
        rows_here, width
    )
    value = jnp.dot(features, w_self, preferred_element_type=jnp.float32)
    value = value + jnp.dot(neigh_mean, w_neigh, preferred_element_type=jnp.float32)
    value = value + bias.astype(jnp.float32)[None, :]
    return jnp.maximum(value, 0.0).astype(jnp.bfloat16)


def solution(mesh):
    in_specs = (
        P(("group", "member"), None),
        P(),
        P(),
        P(),
        P(("group", "member")),
        P(("group", "member"), None),
        P(("group", "member"), None),
        P(("group", "member"), None),
        P(None, ("group", "member")),
        P(("group", "member"), None, None),
    )
    out_specs = P(("group", "member"), None)
    return jax.shard_map(
        per_device, mesh=mesh, in_specs=in_specs, out_specs=out_specs, check_vma=False
    )
```

profile of v0, /device:TPU:1, one launch (start us, length us, event | category | flops | bytes accessed | tf_op | source)
XLA Modules:
  0.0 296.7 jit_solution(11345397366022526329)
XLA Ops:
  6.5 0.9 compare_and_fusion
  8.1 12.9 %gather_fusion.1 = bf16[2048,1024]{1,0:T(8,128)(2,1)} fusion(bf16[1024,1024]{1,0:T(8,128)(2,1)} %param.12, s32[2048]{0:T(1024)S(1)} %broadcast_clamp_fusion), kind=kCustom, calls=%fused_computation.1 | custom fusion | bytes 8396800 | tf_op jit(solution)/shard_map/jit(_take)/gather | solution.py:60
  21.0 3.8 %broadcast_select_fusion = bf16[16,128,1024]{2,1,0:T(8,128)(2,1)} fusion(bf16[16,128,1024]{2,1,0:T(8,128)(2,1)} %bitcast.181, pred[16,128]{1,0:T(8,128)(4,1)S(1)} %compare_and_fusion), kind=kLoop, calls=%fused_computation.229 | loop fusion | flops 2097152 | bytes 8390656 | tf_op jit(solution)/shard_map/jit(_take)/select_n | solution.py:60
  24.8 10.1 %all-to-all-start = ((bf16[16,128,1024]{2,1,0:T(8,128)(2,1)}), bf16[16,128,1024]{2,1,0:T(8,128)(2,1)}, u32[]{:S(2)}, u32[]{:S(2)}) async-start(bf16[16,128,1024]{2,1,0:T(8,128)(2,1)} %broadcast_select_fusion), calls=%async_computation | async-start | bytes 8388608 | tf_op jit(solution)/shard_map/all_to_all | solution.py:63
  35.0 2.4 gather_fusion
  38.3 5.9 %fusion.130 = f32[1024,1024]{1,0:T(8,128)} fusion(bf16[1024,1024]{1,0:T(8,128)(2,1)} %param.12, bf16[1024,1024]{1,0:T(8,128)(2,1)S(1)} %copy-done), kind=kOutput, calls=%fused_computation.241 | convolution fusion | flops 2147483648 | bytes 8388608 | tf_op jit(solution)/shard_map/dot_general | solution.py:80
  44.2 141.6 %all-gather.3.cloned.1.call-done = bf16[256,6,1024]{2,1,0:T(8,128)(2,1)} async-done(((bf16[1,6,1024]{2,1,0:T(8,128)(2,1)}), bf16[256,6,1024]{2,1,0:T(8,128)(2,1)}) %all-gather.3.cloned.1.call-update) | async-done | bytes 3145744 | tf_op jit(solution)/shard_map/all_gather | solution.py:59
  185.8 6.3 %reshape.113 = bf16[1536,1024]{1,0:T(8,128)(2,1)} reshape(bf16[256,6,1024]{2,1,0:T(8,128)(2,1)} %all-gather.3.cloned.1.call-done) | data formatting | bytes 6291456
  192.1 90.6 %while.10 = (s32[]{:T(128)}, bf16[4,256,1024]{2,1,0:T(8,128)(2,1)}, s32[4,256,16]{1,0,2:T(4,128)S(1)}, s32[4,3,256]{2,1,0:T(4,128)}, bf16[1024,1024]{1,0:T(8,128...) while((s32[]{:T(128)}, bf16[4,256,1024]{2,1,0:T(8,128)(2,1)}, ...), condition=%wide.region_4.5_spmd, body=%wide.region_0.4_spmd.sunk | while | flops 2479922944 | bytes 22876868 | solution.py:77
  192.1 0.8 constant_dynamic-slice_fusion.8
  193.7 5.0 %fusion.153 = f32[256,1024]{1,0:T(8,128)S(1)} fusion(bf16[1536,1024]{1,0:T(8,128)(2,1)} %get-tuple-element.437, s32[256]{0:T(256)S(1)} %bitcast.226, s32[256]{0:T(256)S(1)} %bitcast.227, s32[256]{0:T(256)S(1)} %bitcast.228, s32[256]{0:T(256)S(1)} %bitcast.229, s32[256]{0:T(256)S(1)} %bitcast.230, s32[256]{0:T(256)S(1)} %bitcast.231, ...), kind=kOutput, calls=%fused_computation.124.clone.1 | convolution fusion | flops 817889280 | bytes 4204544 | tf_op jit(solution)/shard_map/while/body/eval_jaxpr/dot_general | solution.py:36
  198.9 9.7 %fusion.151 = f32[256,1024]{1,0:T(8,128)S(1)} fusion(bf16[2048,1024]{1,0:T(8,128)(2,1)} %get-tuple-element.439, s32[256]{0:T(256)S(1)} %bitcast.210, s32[256]{0:T(256)S(1)} %bitcast.211, s32[256]{0:T(256)S(1)} %bitcast.212, s32[256]{0:T(256)S(1)} %bitcast.213, s32[256]{0:T(256)S(1)} %bitcast.214, s32[256]{0:T(256)S(1)} %bitcast.215, ...), kind=kOutput, calls=%fused_computation.58.clone.1 | convolution fusion | flops 1107296256 | bytes 5263360 | tf_op jit(solution)/shard_map/while/body/eval_jaxpr/dot_general | solution.py:40
  208.8 6.0 %fusion.155 = bf16[4,256,1024]{2,1,0:T(8,128)(2,1)} fusion(bf16[4,256,1024]{2,1,0:T(8,128)(2,1)} %get-tuple-element.419, s32[]{:T(128)} %get-tuple-element.418, f32[256,1024]{1,0:T(8,128)S(1)} %fusion.151, f32[256,1024]{1,0:T(8,128)S(1)} %fusion.153, bf16[1024,1024]{1,0:T(8,128)(2,1)S(1)} %copy-done.1, f32[256]{0:T(256)S(1)} %add_add_fusion.2, ...), kind=kOutput, calls=%fused_computation.57.clone.1 | convolution fusion | flops 554696704 | bytes 4740608 | tf_op jit(solution)/shard_map/while/body/eval_jaxpr/dot_general | solution.py:34
  214.8 0.8 constant_dynamic-slice_fusion.8
  216.4 5.0 %fusion.153 = f32[256,1024]{1,0:T(8,128)S(1)} fusion(bf16[1536,1024]{1,0:T(8,128)(2,1)} %get-tuple-element.437, s32[256]{0:T(256)S(1)} %bitcast.226, s32[256]{0:T(256)S(1)} %bitcast.227, s32[256]{0:T(256)S(1)} %bitcast.228, s32[256]{0:T(256)S(1)} %bitcast.229, s32[256]{0:T(256)S(1)} %bitcast.230, s32[256]{0:T(256)S(1)} %bitcast.231, ...), kind=kOutput, calls=%fused_computation.124.clone.1 | convolution fusion | flops 817889280 | bytes 4204544 | tf_op jit(solution)/shard_map/while/body/eval_jaxpr/dot_general | solution.py:36
  221.6 9.7 %fusion.151 = f32[256,1024]{1,0:T(8,128)S(1)} fusion(bf16[2048,1024]{1,0:T(8,128)(2,1)} %get-tuple-element.439, s32[256]{0:T(256)S(1)} %bitcast.210, s32[256]{0:T(256)S(1)} %bitcast.211, s32[256]{0:T(256)S(1)} %bitcast.212, s32[256]{0:T(256)S(1)} %bitcast.213, s32[256]{0:T(256)S(1)} %bitcast.214, s32[256]{0:T(256)S(1)} %bitcast.215, ...), kind=kOutput, calls=%fused_computation.58.clone.1 | convolution fusion | flops 1107296256 | bytes 5263360 | tf_op jit(solution)/shard_map/while/body/eval_jaxpr/dot_general | solution.py:40
  231.5 6.0 %fusion.155 = bf16[4,256,1024]{2,1,0:T(8,128)(2,1)} fusion(bf16[4,256,1024]{2,1,0:T(8,128)(2,1)} %get-tuple-element.419, s32[]{:T(128)} %get-tuple-element.418, f32[256,1024]{1,0:T(8,128)S(1)} %fusion.151, f32[256,1024]{1,0:T(8,128)S(1)} %fusion.153, bf16[1024,1024]{1,0:T(8,128)(2,1)S(1)} %copy-done.1, f32[256]{0:T(256)S(1)} %add_add_fusion.2, ...), kind=kOutput, calls=%fused_computation.57.clone.1 | convolution fusion | flops 554696704 | bytes 4740608 | tf_op jit(solution)/shard_map/while/body/eval_jaxpr/dot_general | solution.py:34
  239.0 5.0 %fusion.153 = f32[256,1024]{1,0:T(8,128)S(1)} fusion(bf16[1536,1024]{1,0:T(8,128)(2,1)} %get-tuple-element.437, s32[256]{0:T(256)S(1)} %bitcast.226, s32[256]{0:T(256)S(1)} %bitcast.227, s32[256]{0:T(256)S(1)} %bitcast.228, s32[256]{0:T(256)S(1)} %bitcast.229, s32[256]{0:T(256)S(1)} %bitcast.230, s32[256]{0:T(256)S(1)} %bitcast.231, ...), kind=kOutput, calls=%fused_computation.124.clone.1 | convolution fusion | flops 817889280 | bytes 4204544 | tf_op jit(solution)/shard_map/while/body/eval_jaxpr/dot_general | solution.py:36
  244.2 9.7 %fusion.151 = f32[256,1024]{1,0:T(8,128)S(1)} fusion(bf16[2048,1024]{1,0:T(8,128)(2,1)} %get-tuple-element.439, s32[256]{0:T(256)S(1)} %bitcast.210, s32[256]{0:T(256)S(1)} %bitcast.211, s32[256]{0:T(256)S(1)} %bitcast.212, s32[256]{0:T(256)S(1)} %bitcast.213, s32[256]{0:T(256)S(1)} %bitcast.214, s32[256]{0:T(256)S(1)} %bitcast.215, ...), kind=kOutput, calls=%fused_computation.58.clone.1 | convolution fusion | flops 1107296256 | bytes 5263360 | tf_op jit(solution)/shard_map/while/body/eval_jaxpr/dot_general | solution.py:40
  254.1 6.0 %fusion.155 = bf16[4,256,1024]{2,1,0:T(8,128)(2,1)} fusion(bf16[4,256,1024]{2,1,0:T(8,128)(2,1)} %get-tuple-element.419, s32[]{:T(128)} %get-tuple-element.418, f32[256,1024]{1,0:T(8,128)S(1)} %fusion.151, f32[256,1024]{1,0:T(8,128)S(1)} %fusion.153, bf16[1024,1024]{1,0:T(8,128)(2,1)S(1)} %copy-done.1, f32[256]{0:T(256)S(1)} %add_add_fusion.2, ...), kind=kOutput, calls=%fused_computation.57.clone.1 | convolution fusion | flops 554696704 | bytes 4740608 | tf_op jit(solution)/shard_map/while/body/eval_jaxpr/dot_general | solution.py:34
  261.7 5.0 %fusion.153 = f32[256,1024]{1,0:T(8,128)S(1)} fusion(bf16[1536,1024]{1,0:T(8,128)(2,1)} %get-tuple-element.437, s32[256]{0:T(256)S(1)} %bitcast.226, s32[256]{0:T(256)S(1)} %bitcast.227, s32[256]{0:T(256)S(1)} %bitcast.228, s32[256]{0:T(256)S(1)} %bitcast.229, s32[256]{0:T(256)S(1)} %bitcast.230, s32[256]{0:T(256)S(1)} %bitcast.231, ...), kind=kOutput, calls=%fused_computation.124.clone.1 | convolution fusion | flops 817889280 | bytes 4204544 | tf_op jit(solution)/shard_map/while/body/eval_jaxpr/dot_general | solution.py:36
  266.8 9.7 %fusion.151 = f32[256,1024]{1,0:T(8,128)S(1)} fusion(bf16[2048,1024]{1,0:T(8,128)(2,1)} %get-tuple-element.439, s32[256]{0:T(256)S(1)} %bitcast.210, s32[256]{0:T(256)S(1)} %bitcast.211, s32[256]{0:T(256)S(1)} %bitcast.212, s32[256]{0:T(256)S(1)} %bitcast.213, s32[256]{0:T(256)S(1)} %bitcast.214, s32[256]{0:T(256)S(1)} %bitcast.215, ...), kind=kOutput, calls=%fused_computation.58.clone.1 | convolution fusion | flops 1107296256 | bytes 5263360 | tf_op jit(solution)/shard_map/while/body/eval_jaxpr/dot_general | solution.py:40
  276.7 6.0 %fusion.155 = bf16[4,256,1024]{2,1,0:T(8,128)(2,1)} fusion(bf16[4,256,1024]{2,1,0:T(8,128)(2,1)} %get-tuple-element.419, s32[]{:T(128)} %get-tuple-element.418, f32[256,1024]{1,0:T(8,128)S(1)} %fusion.151, f32[256,1024]{1,0:T(8,128)S(1)} %fusion.153, bf16[1024,1024]{1,0:T(8,128)(2,1)S(1)} %copy-done.1, f32[256]{0:T(256)S(1)} %add_add_fusion.2, ...), kind=kOutput, calls=%fused_computation.57.clone.1 | convolution fusion | flops 554696704 | bytes 4740608 | tf_op jit(solution)/shard_map/while/body/eval_jaxpr/dot_general | solution.py:34
  282.7 7.1 %maximum_convert_fusion = bf16[1024,1024]{1,0:T(8,128)(2,1)} fusion(f32[1024,1024]{1,0:T(8,128)} %fusion.130, f32[1024]{0:T(1024)S(1)} %convert_element_type.147, bf16[1024,1024]{1,0:T(8,128)(2,1)} %bitcast.56, bf16[1024,1024]{1,0:T(8,128)(2,1)} %param.14), kind=kOutput, calls=%fused_computation.228 | convolution fusion | flops 2151677952 | bytes 10489856 | tf_op jit(solution)/shard_map/dot_general | solution.py:81
  (97 shorter events, 7.3 us)
Async XLA Ops:
  6.5 31.8 %copy-start = (bf16[1024,1024]{1,0:T(8,128)(2,1)S(1)}, bf16[1024,1024]{1,0:T(8,128)(2,1)}, u32[]{:S(2)}) copy-start(bf16[1024,1024]{1,0:T(8,128)(2,1)} %param.13) | copy-start | bytes 6291460
  24.8 10.2 %copy-start.5 = (s32[6]{0:T(128)S(1)}, s32[6]{0:T(128)}, u32[]{:S(2)}) copy-start(s32[6]{0:T(128)} %param.16) | copy-start | bytes 76
  24.8 13.4 %copy-start.2 = (s32[1024,16]{0,1:T(8,128)S(1)}, s32[1024,16]{0,1:T(8,128)}, u32[]{:S(2)}) copy-start(s32[1024,16]{0,1:T(8,128)} %param.18) | copy-start | bytes 196612
  24.8 13.4 %copy-start.3 = (s32[1024,16]{0,1:T(8,128)S(1)}, s32[1024,16]{0,1:T(8,128)}, u32[]{:S(2)}) copy-start(s32[1024,16]{0,1:T(8,128)} %param.19) | copy-start | bytes 196612
  24.8 13.5 %copy-start.4 = (bf16[1024]{0:T(1024)(128)(2,1)S(1)}, bf16[1024]{0:T(1024)(128)(2,1)}, u32[]{:S(2)}) copy-start(bf16[1024]{0:T(1024)(128)(2,1)} %param.15) | copy-start | bytes 6148
  24.8 167.3 %all-to-all-start = ((bf16[16,128,1024]{2,1,0:T(8,128)(2,1)}), bf16[16,128,1024]{2,1,0:T(8,128)(2,1)}, u32[]{:S(2)}, u32[]{:S(2)}) async-start(bf16[16,128,1024]{2,1,0:T(8,128)(2,1)} %broadcast_select_fusion), calls=%async_computation | async-start | bytes 8388608 | tf_op jit(solution)/shard_map/all_to_all | solution.py:63
  34.9 150.9 %all-gather.3.cloned.1.call-start = ((), (), s32[]{:S(2)}) async-start(), calls=%async_computation.1 | async-start | bytes 4210688 | tf_op jit(solution)/shard_map/all_gather | solution.py:59
  198.9 9.9 %copy-start.1 = (bf16[1024,1024]{1,0:T(8,128)(2,1)S(1)}, bf16[1024,1024]{1,0:T(8,128)(2,1)}, u32[]{:S(2)}) copy-start(bf16[1024,1024]{1,0:T(8,128)(2,1)} %get-tuple-element.435) | copy-start | bytes 6291460 | tf_op jit(solution)/shard_map/while
  221.5 9.9 %copy-start.1 = (bf16[1024,1024]{1,0:T(8,128)(2,1)S(1)}, bf16[1024,1024]{1,0:T(8,128)(2,1)}, u32[]{:S(2)}) copy-start(bf16[1024,1024]{1,0:T(8,128)(2,1)} %get-tuple-element.435) | copy-start | bytes 6291460 | tf_op jit(solution)/shard_map/while
  244.2 9.9 %copy-start.1 = (bf16[1024,1024]{1,0:T(8,128)(2,1)S(1)}, bf16[1024,1024]{1,0:T(8,128)(2,1)}, u32[]{:S(2)}) copy-start(bf16[1024,1024]{1,0:T(8,128)(2,1)} %get-tuple-element.435) | copy-start | bytes 6291460 | tf_op jit(solution)/shard_map/while
  266.8 9.9 %copy-start.1 = (bf16[1024,1024]{1,0:T(8,128)(2,1)S(1)}, bf16[1024,1024]{1,0:T(8,128)(2,1)}, u32[]{:S(2)}) copy-start(bf16[1024,1024]{1,0:T(8,128)(2,1)} %get-tuple-element.435) | copy-start | bytes 6291460 | tf_op jit(solution)/shard_map/while
Sparse Core Ops, SparseCore 0:
  39.5 146.2 all-gather.2
where the time goes:
time: 298 us; the launch traced here: 297 us
  waiting for transfers between devices  142 us (48%)
  matrix products  95.8 us (32%)
  local copies, waits for them, and re-layouts  28.7 us (10%)
  between operations  13.5 us (5%)
  starting transfers between devices  10.2 us (3%)
  other arithmetic  6.4 us (2%)
    all_gather x1, waiting for transfers between devices, per_device(): lax.all_gather(mine, ('group', 'member'), axis=0, tiled=True)  142 us
    dot_general x4, matrix products, block_mean(): jnp.dot(halo_counts, neighbour_positions, preferred_element_type=jnp.floa...  38.9 us
    dot_general x4, matrix products, block_mean(): jnp.dot(local_counts, self_features, preferred_element_type=jnp.float32)  23.9 us
    dot_general x4, matrix products, block_mean(): jnp.dot(hub_counts, hub_lookup_matrix, preferred_element_type=jnp.float32)  20.1 us
    gather x1, local copies, waits for them, and re-layouts, per_device(): jnp.take(features, send_rows.reshape(peers * caps), axis=0)  12.9 us
    all_to_all x1, starting transfers between devices, per_device(): lax.all_to_all(outgoing, 'member', split_axis=0, concat_axis=0, tiled=True)  10.1 us
    dot_general x1, matrix products, per_device(): jnp.dot(neigh_mean, w_neigh, preferred_element_type=jnp.float32)  7.11 us
    unnamed x11, local copies, waits for them, and re-layouts  6.35 us
  transfers between devices with their start and end apart: 2, of which 1 were waited for; matrix products, arithmetic and copies ran while one was open for 5% of the time, Pallas kernels for 0%

commit v1 on v0

v1 whole, which is shorter than its diff:
```python
import functools

import jax
import jax.numpy as jnp
from jax import lax
from jax.experimental import pallas as pl
from jax.experimental.pallas import tpu as pltpu
from jax.sharding import PartitionSpec as P

MESH = pl.DeviceIdType.MESH
BF16 = jnp.bfloat16
F32 = jnp.float32
I32 = jnp.int32
CAP = 128
ZS = 8
GROUPS = 16
HUB = 6
HUBP = 8
HUBZ = ZS * HUB
HALF = GROUPS * HUBZ
CHUNK = 256
STEPS = (0, 4, 3, 5, 2, 6, 1, 7)


def iota(shape, dim):
    return lax.broadcasted_iota(I32, shape, dim)


def spread(row):
    return jnp.broadcast_to(row, (128, 128)).T


def dot(a, b):
    return jnp.dot(a, b, preferred_element_type=F32)


def kernel(
    hub_rows,
    feat_hbm,
    ws_hbm,
    wn_hbm,
    bias_ref,
    hubn_hbm,
    localn_hbm,
    halon_hbm,
    deg_ref,
    send_ref,
    out_hbm,
    feat,
    ws,
    wn,
    hubn,
    localn,
    halon,
    sendbuf,
    recv,
    hubz,
    hubtab,
    cnt_local,
    cnt_hub,
    cnt_halo,
    wide,
    inv,
    acc,
    own,
    outbuf,
    in_sem,
    out_sem,
    self_sem,
    ss,
    rs,
    zss,
    zrs,
    pss,
    prs,
    css,
    crs,
):
    g = lax.axis_index("group")
    m = lax.axis_index("member")
    z = m // 2
    c = lax.rem(m, 2)
    rows = feat.shape[0]

    def peer(dz, dc):
        return lax.rem(z + dz, ZS) * 2 + lax.rem(c + dc, 2)

    loads = [
        pltpu.make_async_copy(src, dst, in_sem.at[i])
        for i, (src, dst) in enumerate(
            (
                (feat_hbm, feat),
                (ws_hbm, ws),
                (localn_hbm, localn),
                (halon_hbm, halon),
                (hubn_hbm, hubn),
                (wn_hbm, wn),
            )
        )
    ]
    for load in loads:
        load.start()

    barrier = pltpu.get_barrier_semaphore()
    for o in range(1, 2 * ZS):
        pl.semaphore_signal(barrier, inc=1, device_id=(g, peer(o // 2, o % 2)), device_id_type=MESH)
    for dg in range(1, GROUPS):
        pl.semaphore_signal(barrier, inc=1, device_id=(lax.rem(g + dg, GROUPS), m), device_id_type=MESH)

    loads[0].wait()
    lane = iota((128, 128), 1)

    hot = jnp.zeros((16, rows), F32)
    for r in range(HUB):
        hot = jnp.where((iota((16, rows), 0) == r) & (iota((16, rows), 1) == hub_rows[r]), 1.0, hot)
    hubz[0] = dot(hot.astype(BF16), feat[...])[:HUBP].astype(BF16)

    def pick(i, carry):
        parts = []
        for half in range(CHUNK // CAP):
            t = spread(send_ref[0, pl.ds(i * (CHUNK // CAP) + half, 1), :])
            parts.append(
                jnp.concatenate(
                    [jnp.where(t == lane + 128 * b, 1.0, 0.0).astype(BF16) for b in range(rows // 128)],
                    axis=1,
                )
            )
        at = pl.ds(pl.multiple_of(i * CHUNK, CHUNK), CHUNK)
        sendbuf[at, :] = dot(jnp.concatenate(parts, axis=0), feat[...]).astype(BF16)
        return carry

    lax.fori_loop(0, 2 * ZS * CAP // CHUNK, pick, 0)

    pl.semaphore_wait(barrier, 2 * ZS - 1 + GROUPS - 1)

    zcopies = []
    for dz in range(1, ZS):
        zcopies.append(
            pltpu.make_async_remote_copy(
                src_ref=hubz.at[0],
                dst_ref=hubz.at[dz],
                send_sem=zss.at[dz],
                recv_sem=zrs.at[dz],
                device_id=(g, peer(dz, 0)),
                device_id_type=MESH,
            )
        )
        zcopies[-1].start()
    copies = {}
    for t, dz in enumerate(STEPS):
        for dc in range(2):
            if t == 0 and dc == 0:
                continue
            s = 2 * t + dc
            to = peer(dz, dc)
            copies[s] = pltpu.make_async_remote_copy(
                src_ref=sendbuf.at[pl.ds(pl.multiple_of(to * CAP, CAP), CAP), :],
                dst_ref=recv.at[pl.ds(s * CAP, CAP), :],
                send_sem=ss.at[s],
                recv_sem=rs.at[s],
                device_id=(g, to),
                device_id_type=MESH,
            )
            copies[s].start()
    keep = pltpu.make_async_copy(
        sendbuf.at[pl.ds(pl.multiple_of(m * CAP, CAP), CAP), :], recv.at[pl.ds(0, CAP), :], self_sem
    )
    keep.start()

    loads[1].wait()
    bias = bias_ref[...].astype(F32).reshape(1, ws.shape[1])

    def own_part(i, carry):
        at = pl.ds(pl.multiple_of(i * CHUNK, CHUNK), CHUNK)
        own[at, :] = dot(feat[at, :], ws[...]) + bias
        return carry

    lax.fori_loop(0, rows // CHUNK, own_part, 0)

    def counts(indices, which, blocks, places, table):
        width = indices.shape[0]

        def some_rows(i, carry):
            at = pl.ds(pl.multiple_of(i * 128, 128), 128)
            deg = deg_ref[pl.ds(which, 1), at]
            for k in range(width):
                wide[k] = spread(jnp.where(k < deg, indices[pl.ds(k, 1), at], -1))

            def some_columns(b, carry):
                place = places(b)
                tally = jnp.zeros((128, 128), F32)
                for k in range(width):
                    tally = tally + jnp.where(wide[k] == place, 1.0, 0.0)
                table[at, pl.ds(pl.multiple_of(b * 128, 128), 128)] = tally.astype(BF16)
                return carry

            return lax.fori_loop(0, blocks, some_columns, carry)

        lax.fori_loop(0, rows // 128, some_rows, 0)

    def add(table, first, width, values, start):
        def some_rows(i, carry):
            at = pl.ds(pl.multiple_of(i * CHUNK, CHUNK), CHUNK)
            part = dot(table[at, first : first + width], values[first : first + width, :])
            acc[at, :] = part if start else acc[at, :] + part
            return carry

        lax.fori_loop(0, rows // CHUNK, some_rows, 0)

    loads[2].wait()
    counts(localn, 0, rows // 128, lambda b: lane + 128 * b, cnt_local)

    for copy in zcopies:
        copy.wait()
    q = iota((HUBZ, ZS * HUBP), 1)
    r = jnp.bitwise_and(q, HUBP - 1)
    target = jnp.bitwise_and(z + ZS - q // HUBP, ZS - 1) * HUB + r
    sel = jnp.where((iota((HUBZ, ZS * HUBP), 0) == target) & (r < HUB), 1.0, 0.0).astype(BF16)
    stacked = hubz[...].astype(F32).reshape(ZS * HUBP, feat.shape[1]).astype(BF16)
    mine = hubtab.at[pl.ds(pl.multiple_of(g * HUBZ, 16), HUBZ), :]
    mine[...] = dot(sel, stacked).astype(BF16)

    add(cnt_local, 0, rows, feat, True)

    pcopies = []
    for dg in range(1, GROUPS):
        pcopies.append(
            pltpu.make_async_remote_copy(
                src_ref=mine,
                dst_ref=mine,
                send_sem=pss.at[dg],
                recv_sem=prs.at[dg],
                device_id=(lax.rem(g + dg, GROUPS), m),
                device_id_type=MESH,
            )
        )
        pcopies[-1].start()

    def halo_place(b):
        t = b // 2
        dz = jnp.where(t == 0, 0, jnp.where(lax.rem(t, 2) == 1, 4 + t // 2, 4 - t // 2))
        j = lax.rem(z - dz + ZS, ZS) * 2 + lax.rem(c + lax.rem(b, 2), 2)
        return lane + j * CAP

    loads[3].wait()
    counts(halon, 2, 2 * ZS, halo_place, cnt_halo)

    for copy in pcopies:
        copy.wait()
    cross = pltpu.make_async_remote_copy(
        src_ref=hubtab.at[pl.ds(0, HALF), :],
        dst_ref=hubtab.at[pl.ds(HALF, HALF), :],
        send_sem=css,
        recv_sem=crs,
        device_id=(g, peer(0, 1)),
        device_id_type=MESH,
    )
    cross.start()

    def hub_place(b):
        half = b // (HALF // 128)
        p = lane + 128 * lax.rem(b, HALF // 128)
        group = p // HUBZ
        inner = p - group * HUBZ
        chip = inner // HUB
        core = lax.rem(c + half, 2)
        return ((group * ZS + chip) * 2 + core) * HUB + inner - chip * HUB

    loads[4].wait()
    counts(hubn, 1, 2 * HALF // 128, hub_place, cnt_hub)

    def inverse(i, carry):
        at = pl.ds(pl.multiple_of(i * 128, 128), 128)
        total = deg_ref[0:1, at] + deg_ref[1:2, at] + deg_ref[2:3, at]
        inv[at, :] = 1.0 / jnp.maximum(spread(total).astype(F32), 1.0)
        return carry

    lax.fori_loop(0, rows // 128, inverse, 0)

    cross.wait()
    add(cnt_hub, 0, 2 * HALF, hubtab, False)

    keep.wait()
    copies[1].wait()
    for t in range(1, 6):
        copies[2 * t].wait()
        copies[2 * t + 1].wait()
        if t % 2 == 1:
            add(cnt_halo, (t - 1) * 2 * CAP, 4 * CAP, recv, False)

    loads[5].wait()
    for s in range(12, 16):
        copies[s].wait()

    def last(i, carry):
        at = pl.ds(pl.multiple_of(i * CHUNK, CHUNK), CHUNK)
        total = acc[at, :] + dot(cnt_halo[at, 12 * CAP :], recv[12 * CAP :, :])
        scale = inv[at, :]
        mean = (total * jnp.concatenate([scale] * (total.shape[1] // 128), axis=1)).astype(BF16)
        value = own[at, :] + dot(mean, wn[...])
        outbuf[at, :] = jnp.maximum(value, 0.0).astype(BF16)
        return carry

    lax.fori_loop(0, rows // CHUNK, last, 0)
    store = pltpu.make_async_copy(outbuf, out_hbm, out_sem)
    store.start()
    store.wait()


def per_device(
    features, w_self, w_neigh, bias, hub_rows, hub_nbrs, local_nbrs, halo_nbrs, degrees, send_rows
):
    rows, width = features.shape
    wide_out = w_self.shape[1]
    vmem = pl.BlockSpec(memory_space=pltpu.VMEM)
    hbm = pl.BlockSpec(memory_space=pl.ANY)
    dma = pltpu.SemaphoreType.DMA
    return pl.pallas_call(
        kernel,
        out_shape=jax.ShapeDtypeStruct((rows, wide_out), BF16),
        in_specs=[
            pl.BlockSpec(memory_space=pltpu.SMEM),
            hbm,
            hbm,
            hbm,
            vmem,
            hbm,
            hbm,
            hbm,
            vmem,
            vmem,
        ],
        out_specs=hbm,
        scratch_shapes=[
            pltpu.VMEM((rows, width), BF16),
            pltpu.VMEM(w_self.shape, BF16),
            pltpu.VMEM(w_neigh.shape, BF16),
            pltpu.VMEM(hub_nbrs.shape[::-1], I32),
            pltpu.VMEM(local_nbrs.shape[::-1], I32),
            pltpu.VMEM(halo_nbrs.shape[::-1], I32),
            pltpu.VMEM((2 * ZS * CAP, width), BF16),
            pltpu.VMEM((2 * ZS * CAP, width), BF16),
            pltpu.VMEM((ZS, HUBP, width), BF16),
            pltpu.VMEM((2 * HALF, width), BF16),
            pltpu.VMEM((rows, rows), BF16),
            pltpu.VMEM((rows, 2 * HALF), BF16),
            pltpu.VMEM((rows, 2 * ZS * CAP), BF16),
            pltpu.VMEM((16, 128, 128), I32),
            pltpu.VMEM((rows, 128), F32),
            pltpu.VMEM((rows, width), F32),
            pltpu.VMEM((rows, wide_out), F32),
            pltpu.VMEM((rows, wide_out), BF16),
            dma((6,)),
            dma,
            dma,
            dma((16,)),
            dma((16,)),
            dma((ZS,)),
            dma((ZS,)),
            dma((GROUPS,)),
            dma((GROUPS,)),
            dma,
            dma,
        ],
        compiler_params=pltpu.CompilerParams(
            collective_id=0, has_side_effects=True, vmem_limit_bytes=60 << 20
        ),
    )(
        hub_rows,
        features,
        w_self,
        w_neigh,
        bias,
        hub_nbrs.T,
        local_nbrs.T,
        halo_nbrs.T,
        degrees,
        send_rows,
    )


def solution(mesh):
    in_specs = (
        P(("group", "member"), None),
        P(),
        P(),
        P(),
        P(("group", "member")),
        P(("group", "member"), None),
        P(("group", "member"), None),
        P(("group", "member"), None),
        P(None, ("group", "member")),
        P(("group", "member"), None, None),
    )
    out_specs = P(("group", "member"), None)
    return jax.shard_map(
        per_device, mesh=mesh, in_specs=in_specs, out_specs=out_specs, check_vma=False
    )
```

time: 298 us -> 118 us (0.40)
  waiting for transfers between devices: 142 us -> 0 us
  Pallas kernels: 0 us -> 115 us
  matrix products: 95.8 us -> 0 us
  local copies, waits for them, and re-layouts: 28.7 us -> 3.08 us
  between operations: 13.5 us -> 0.01 us
  starting transfers between devices: 10.2 us -> 0 us
  other arithmetic: 6.4 us -> 0 us
    all_gather x1 -> x0, waiting for transfers between devices: 142 us -> none  [per_device(): lax.all_gather(mine, ('group', 'member'), axis=0, tiled=True)]
    pallas_call x0 -> x1, Pallas kernels: none -> 115 us  [per_device(): pl.pallas_call(kernel, out_shape=jax.ShapeDtypeStruct((rows, wide_out), B...]
    dot_general x14 -> x0, matrix products: 95.8 us -> none  [the longest x4 38.9 us: block_mean(): jnp.dot(halo_counts, neighbour_positions, preferred_element_type=jnp.floa...]
    gather x2 -> x0, local copies, waits for them, and re-layouts: 15.3 us -> none  [the longest x1 12.9 us: per_device(): jnp.take(features, send_rows.reshape(peers * caps), axis=0)]
    all_to_all x1 -> x0, starting transfers between devices: 10.1 us -> none  [per_device(): lax.all_to_all(outgoing, 'member', split_axis=0, concat_axis=0, tiled=True)]
    select_n x3 -> x0, other arithmetic: 4.55 us -> none  [the longest x2 4.54 us: per_device(): jnp.take(features, send_rows.reshape(peers * caps), axis=0)]
    slice x28 -> x0, local copies, waits for them, and re-layouts: 4.02 us -> none  [the longest x4 3.21 us: block_mean(): local_valid_mask = jnp.arange(klocal)[None, :] < deg[0][:, None]]
    unnamed x11 -> x1, local copies, waits for them, and re-layouts: 6.35 us -> 3.08 us
  transfers between devices with their start and end apart: 2 -> 0, of which waited for: 1 -> 0; matrix products, arithmetic and copies ran while one was open for 5% -> 0% of each run, Pallas kernels for 0% -> 0%
where the time goes in v1:
time: 118 us
  Pallas kernels  115 us (97%)
  local copies, waits for them, and re-layouts  3.08 us (3%)
    pallas_call x1, Pallas kernels, per_device(): pl.pallas_call(kernel, out_shape=jax.ShapeDtypeStruct((rows, wide_out), B...  115 us
    unnamed x1, local copies, waits for them, and re-layouts  3.08 us

profile of v1, /device:TPU:1, one launch (start us, length us, event | category | flops | bytes accessed | tf_op | source)
XLA Modules:
  0.0 118.2 jit_solution(3425800008547343461)
XLA Ops:
  0.0 115.1 %shard_map.100 = bf16[1024,1024]{1,0:T(8,128)(2,1)} custom-call(s32[6]{0:T(128)} %hub_rows.1, bf16[1024,1024]{1,0:T(8,128)(2,1)} %feat_hbm.1, bf16[1024,1024]{1,0:T(8,128)(2,1)} %ws_hbm.1, bf16[1024,1024]{1,0:T(8,128)(2,1)} %wn_hbm.1, bf16[1024]{0:T(1024)(128)(2,1)} %bias_ref.1, s32[8,1024]{1,0:T(8,128)} %bitcast.5, s32[16,1024]{1,0:T(8,128)} %bitcast.3, ...), custom_call_target="tpu_custom_call" | custom-call | tf_op jit(solution)/shard_map/pallas_call | solution.py:318
  115.2 3.1 %copy.12 = bf16[1024,1024]{1,0:T(8,128)(2,1)} copy(bf16[1024,1024]{1,0:T(8,128)(2,1)} %shard_map.100) | data formatting | bytes 4194304

commit v2 on v1

--- a/solution.py
+++ b/solution.py
@@ -45,7 +45,7 @@
     halon_hbm,
     deg_ref,
     send_ref,
-    out_hbm,
+    out_ref,
     feat,
     ws,
     wn,
@@ -63,9 +63,7 @@
     inv,
     acc,
     own,
-    outbuf,
     in_sem,
-    out_sem,
     self_sem,
     ss,
     rs,
@@ -81,6 +79,7 @@
     z = m // 2
     c = lax.rem(m, 2)
     rows = feat.shape[0]
+    split = feat.shape[1] * 3 // 4
 
     def peer(dz, dc):
         return lax.rem(z + dz, ZS) * 2 + lax.rem(c + dc, 2)
@@ -115,21 +114,21 @@
         hot = jnp.where((iota((16, rows), 0) == r) & (iota((16, rows), 1) == hub_rows[r]), 1.0, hot)
     hubz[0] = dot(hot.astype(BF16), feat[...])[:HUBP].astype(BF16)
 
-    def pick(i, carry):
+    def pick(t):
         parts = []
-        for half in range(CHUNK // CAP):
-            t = spread(send_ref[0, pl.ds(i * (CHUNK // CAP) + half, 1), :])
+        for dc in range(2):
+            row = spread(send_ref[0, pl.ds(peer(STEPS[t], dc), 1), :])
             parts.append(
                 jnp.concatenate(
-                    [jnp.where(t == lane + 128 * b, 1.0, 0.0).astype(BF16) for b in range(rows // 128)],
+                    [jnp.where(row == lane + 128 * b, 1.0, 0.0).astype(BF16) for b in range(rows // 128)],
                     axis=1,
                 )
             )
-        at = pl.ds(pl.multiple_of(i * CHUNK, CHUNK), CHUNK)
+        at = pl.ds(2 * t * CAP, 2 * CAP)
         sendbuf[at, :] = dot(jnp.concatenate(parts, axis=0), feat[...]).astype(BF16)
-        return carry
-
-    lax.fori_loop(0, 2 * ZS * CAP // CHUNK, pick, 0)
+
+    for t in range(1, 5):
+        pick(t)
 
     pl.semaphore_wait(barrier, 2 * ZS - 1 + GROUPS - 1)
 
@@ -147,24 +146,39 @@
         )
         zcopies[-1].start()
     copies = {}
-    for t, dz in enumerate(STEPS):
-        for dc in range(2):
-            if t == 0 and dc == 0:
-                continue
-            s = 2 * t + dc
-            to = peer(dz, dc)
-            copies[s] = pltpu.make_async_remote_copy(
-                src_ref=sendbuf.at[pl.ds(pl.multiple_of(to * CAP, CAP), CAP), :],
-                dst_ref=recv.at[pl.ds(s * CAP, CAP), :],
-                send_sem=ss.at[s],
-                recv_sem=rs.at[s],
-                device_id=(g, to),
-                device_id_type=MESH,
-            )
-            copies[s].start()
-    keep = pltpu.make_async_copy(
-        sendbuf.at[pl.ds(pl.multiple_of(m * CAP, CAP), CAP), :], recv.at[pl.ds(0, CAP), :], self_sem
-    )
+
+    def send(t, dc, part, columns):
+        at = (pl.ds((2 * t + dc) * CAP, CAP), columns)
+        copy = pltpu.make_async_remote_copy(
+            src_ref=sendbuf.at[at],
+            dst_ref=recv.at[at],
+            send_sem=ss.at[part, 2 * t + dc],
+            recv_sem=rs.at[part, 2 * t + dc],
+            device_id=(g, peer(STEPS[t], dc)),
+            device_id_type=MESH,
+        )
+        copies[t, dc, part] = copy
+        copy.start()
+
+    head, tail = pl.ds(0, split), pl.ds(split, feat.shape[1] - split)
+    both = pl.ds(0, feat.shape[1])
+    for t in (1, 2, 3):
+        send(t, 0, 0, both)
+        send(t, 1, 0, both)
+    pick(5)
+    send(4, 0, 0, both)
+    send(4, 1, 0, both)
+    pick(6)
+    send(5, 0, 0, both)
+    send(5, 1, 0, both)
+    pick(7)
+    pick(0)
+    for part, columns in enumerate((head, tail)):
+        for t in (6, 7):
+            send(t, 0, part, columns)
+            send(t, 1, part, columns)
+    send(0, 1, 0, both)
+    keep = pltpu.make_async_copy(sendbuf.at[pl.ds(0, CAP), :], recv.at[pl.ds(0, CAP), :], self_sem)
     keep.start()
 
     loads[1].wait()
@@ -281,30 +295,42 @@
     add(cnt_hub, 0, 2 * HALF, hubtab, False)
 
     keep.wait()
-    copies[1].wait()
+    copies[0, 1, 0].wait()
     for t in range(1, 6):
-        copies[2 * t].wait()
-        copies[2 * t + 1].wait()
+        copies[t, 0, 0].wait()
+        copies[t, 1, 0].wait()
         if t % 2 == 1:
             add(cnt_halo, (t - 1) * 2 * CAP, 4 * CAP, recv, False)
 
     loads[5].wait()
-    for s in range(12, 16):
-        copies[s].wait()
-
-    def last(i, carry):
+
+    def last_blocks(i, columns):
         at = pl.ds(pl.multiple_of(i * CHUNK, CHUNK), CHUNK)
-        total = acc[at, :] + dot(cnt_halo[at, 12 * CAP :], recv[12 * CAP :, :])
-        scale = inv[at, :]
-        mean = (total * jnp.concatenate([scale] * (total.shape[1] // 128), axis=1)).astype(BF16)
-        value = own[at, :] + dot(mean, wn[...])
-        outbuf[at, :] = jnp.maximum(value, 0.0).astype(BF16)
+        total = acc[at, columns] + dot(cnt_halo[at, 12 * CAP :], recv[12 * CAP :, columns])
+        mean = total * jnp.concatenate([inv[at, :]] * (total.shape[1] // 128), axis=1)
+        return at, own[at, :] + dot(mean.astype(BF16), wn[columns, :])
+
+    for t in (6, 7):
+        copies[t, 0, 0].wait()
+        copies[t, 1, 0].wait()
+
+    def first_columns(i, carry):
+        at, value = last_blocks(i, head)
+        own[at, :] = value
         return carry
 
-    lax.fori_loop(0, rows // CHUNK, last, 0)
-    store = pltpu.make_async_copy(outbuf, out_hbm, out_sem)
-    store.start()
-    store.wait()
+    lax.fori_loop(0, rows // CHUNK, first_columns, 0)
+
+    for t in (6, 7):
+        copies[t, 0, 1].wait()
+        copies[t, 1, 1].wait()
+
+    def last_columns(i, carry):
+        at, value = last_blocks(i, tail)
+        out_ref[at, :] = jnp.maximum(value, 0.0).astype(BF16)
+        return carry
+
+    lax.fori_loop(0, rows // CHUNK, last_columns, 0)
 
 
 def per_device(
@@ -317,7 +343,7 @@
     dma = pltpu.SemaphoreType.DMA
     return pl.pallas_call(
         kernel,
-        out_shape=jax.ShapeDtypeStruct((rows, wide_out), BF16),
+        out_shape=pltpu.VMEM((rows, wide_out), BF16),
         in_specs=[
             pl.BlockSpec(memory_space=pltpu.SMEM),
             hbm,
@@ -330,7 +356,7 @@
             vmem,
             vmem,
         ],
-        out_specs=hbm,
+        out_specs=vmem,
         scratch_shapes=[
             pltpu.VMEM((rows, width), BF16),
             pltpu.VMEM(w_self.shape, BF16),
@@ -349,12 +375,10 @@
             pltpu.VMEM((rows, 128), F32),
             pltpu.VMEM((rows, width), F32),
             pltpu.VMEM((rows, wide_out), F32),
-            pltpu.VMEM((rows, wide_out), BF16),
             dma((6,)),
             dma,
-            dma,
-            dma((16,)),
-            dma((16,)),
+            dma((2, 16)),
+            dma((2, 16)),
             dma((ZS,)),
             dma((ZS,)),
             dma((GROUPS,)),
@@ -363,7 +387,7 @@
             dma,
         ],
         compiler_params=pltpu.CompilerParams(
-            collective_id=0, has_side_effects=True, vmem_limit_bytes=60 << 20
+            collective_id=0, has_side_effects=True, vmem_limit_bytes=56 << 20
         ),
     )(
         hub_rows,

time: 118 us -> 113 us (0.958)
  Pallas kernels: 115 us -> 111 us
  local copies, waits for them, and re-layouts: 3.08 us -> 1.32 us
    pallas_call x1, Pallas kernels: 115 us -> 111 us  [per_device(): pl.pallas_call(kernel, out_shape=pltpu.VMEM((rows, wide_out), BF16), in_s...]
    unnamed x1, local copies, waits for them, and re-layouts: 3.08 us -> 1.32 us
where the time goes in v2:
time: 113 us
  Pallas kernels  111 us (98%)
  local copies, waits for them, and re-layouts  1.32 us (1%)
    pallas_call x1, Pallas kernels, per_device(): pl.pallas_call(kernel, out_shape=pltpu.VMEM((rows, wide_out), BF16), in_s...  111 us

profile of v2, /device:TPU:1, one launch (start us, length us, event | category | flops | bytes accessed | tf_op | source)
XLA Modules:
  0.0 112.5 jit_solution(16514656582509772959)
XLA Ops:
  0.0 111.2 %shard_map.100 = bf16[1024,1024]{1,0:T(8,128)(2,1)S(1)} custom-call(s32[6]{0:T(128)} %hub_rows.1, bf16[1024,1024]{1,0:T(8,128)(2,1)} %feat_hbm.1, bf16[1024,1024]{1,0:T(8,128)(2,1)} %ws_hbm.1, bf16[1024,1024]{1,0:T(8,128)(2,1)} %wn_hbm.1, bf16[1024]{0:T(1024)(128)(2,1)} %bias_ref.1, s32[8,1024]{1,0:T(8,128)} %bitcast.5, s32[16,1024]{1,0:T(8,128)} %bitcast.3, ...), custom_call_target="tpu_custom_call" | custom-call | tf_op jit(solution)/shard_map/pallas_call | solution.py:344
  111.2 1.3 %copy.12 = bf16[1024,1024]{1,0:T(8,128)(2,1)} copy(bf16[1024,1024]{1,0:T(8,128)(2,1)S(1)} %shard_map.100) | data formatting | bytes 4194304

commit v3 on v2

--- a/solution.py
+++ b/solution.py
@@ -14,8 +14,8 @@
 CAP = 128
 ZS = 8
 GROUPS = 16
+SIDE = 4
 HUB = 6
-HUBP = 8
 HUBZ = ZS * HUB
 HALF = GROUPS * HUBZ
 CHUNK = 256
@@ -71,6 +71,8 @@
     zrs,
     pss,
     prs,
+    yss,
+    yrs,
     css,
     crs,
 ):
@@ -83,6 +85,12 @@
 
     def peer(dz, dc):
         return lax.rem(z + dz, ZS) * 2 + lax.rem(c + dc, 2)
+
+    def beside(step):
+        return g // SIDE * SIDE + lax.rem(g + step, SIDE)
+
+    def above(step):
+        return lax.rem(g + step * SIDE, GROUPS)
 
     loads = [
         pltpu.make_async_copy(src, dst, in_sem.at[i])
@@ -103,16 +111,26 @@
     barrier = pltpu.get_barrier_semaphore()
     for o in range(1, 2 * ZS):
         pl.semaphore_signal(barrier, inc=1, device_id=(g, peer(o // 2, o % 2)), device_id_type=MESH)
-    for dg in range(1, GROUPS):
-        pl.semaphore_signal(barrier, inc=1, device_id=(lax.rem(g + dg, GROUPS), m), device_id_type=MESH)
+    for step in range(1, SIDE):
+        for to in (beside(step), above(step)):
+            pl.semaphore_signal(barrier, inc=1, device_id=(to, m), device_id_type=MESH)
 
     loads[0].wait()
     lane = iota((128, 128), 1)
-
-    hot = jnp.zeros((16, rows), F32)
-    for r in range(HUB):
-        hot = jnp.where((iota((16, rows), 0) == r) & (iota((16, rows), 1) == hub_rows[r]), 1.0, hot)
-    hubz[0] = dot(hot.astype(BF16), feat[...])[:HUBP].astype(BF16)
+    column = iota((1, 128), 1)
+
+    blocks = feat.shape[1] // 128
+    p = iota((HUBZ, rows), 0)
+    r = p - p // HUB * HUB
+    hot = jnp.zeros((HUBZ, rows), F32)
+    for k in range(HUB):
+        hot = jnp.where((r == k) & (iota((HUBZ, rows), 1) == hub_rows[k]), 1.0, hot)
+    repeated = dot(hot.astype(BF16), feat[...])
+    block = iota((HUBZ, 128), 0) // HUB
+    packed = jnp.zeros((HUBZ, 128), F32)
+    for b in range(blocks):
+        packed = jnp.where(block == b, repeated[:, 128 * b : 128 * (b + 1)], packed)
+    hubz[0] = packed.astype(BF16)
 
     def pick(t):
         parts = []
@@ -130,7 +148,7 @@
     for t in range(1, 5):
         pick(t)
 
-    pl.semaphore_wait(barrier, 2 * ZS - 1 + GROUPS - 1)
+    pl.semaphore_wait(barrier, 2 * ZS - 1 + 2 * (SIDE - 1))
 
     zcopies = []
     for dz in range(1, ZS):
@@ -162,15 +180,14 @@
 
     head, tail = pl.ds(0, split), pl.ds(split, feat.shape[1] - split)
     both = pl.ds(0, feat.shape[1])
-    for t in (1, 2, 3):
+    for t in (1, 2):
         send(t, 0, 0, both)
         send(t, 1, 0, both)
     pick(5)
-    send(4, 0, 0, both)
-    send(4, 1, 0, both)
     pick(6)
-    send(5, 0, 0, both)
-    send(5, 1, 0, both)
+    for t in (3, 4, 5):
+        send(t, 0, 0, both)
+        send(t, 1, 0, both)
     pick(7)
     pick(0)
     for part, columns in enumerate((head, tail)):
@@ -191,7 +208,7 @@
 
     lax.fori_loop(0, rows // CHUNK, own_part, 0)
 
-    def counts(indices, which, blocks, places, table):
+    def counts(indices, which, first, end, places, table):
         width = indices.shape[0]
 
         def some_rows(i, carry):
@@ -208,7 +225,7 @@
                 table[at, pl.ds(pl.multiple_of(b * 128, 128), 128)] = tally.astype(BF16)
                 return carry
 
-            return lax.fori_loop(0, blocks, some_columns, carry)
+            return lax.fori_loop(first, end, some_columns, carry)
 
         lax.fori_loop(0, rows // 128, some_rows, 0)
 
@@ -222,44 +239,82 @@
         lax.fori_loop(0, rows // CHUNK, some_rows, 0)
 
     loads[2].wait()
-    counts(localn, 0, rows // 128, lambda b: lane + 128 * b, cnt_local)
+    counts(localn, 0, 0, rows // 128, lambda b: column + 128 * b, cnt_local)
 
     for copy in zcopies:
         copy.wait()
-    q = iota((HUBZ, ZS * HUBP), 1)
-    r = jnp.bitwise_and(q, HUBP - 1)
-    target = jnp.bitwise_and(z + ZS - q // HUBP, ZS - 1) * HUB + r
-    sel = jnp.where((iota((HUBZ, ZS * HUBP), 0) == target) & (r < HUB), 1.0, 0.0).astype(BF16)
-    stacked = hubz[...].astype(F32).reshape(ZS * HUBP, feat.shape[1]).astype(BF16)
+    q = iota((HUBZ, ZS * HUBZ), 1)
+    distance = q // HUBZ
+    inner = q - distance * HUBZ
+    block = inner // HUB
+    target = jnp.bitwise_and(z + ZS - distance, ZS - 1) * HUB + inner - block * HUB
+    right = iota((HUBZ, ZS * HUBZ), 0) == target
+    stacked = hubz[...].reshape(ZS * HUBZ, 128)
     mine = hubtab.at[pl.ds(pl.multiple_of(g * HUBZ, 16), HUBZ), :]
-    mine[...] = dot(sel, stacked).astype(BF16)
+    for b in range(blocks):
+        sel = jnp.where(right & (block == b), 1.0, 0.0).astype(BF16)
+        mine[:, 128 * b : 128 * (b + 1)] = dot(sel, stacked).astype(BF16)
+
+    def share(held, towards, send_sems, recv_sems):
+        shared = []
+        for step in range(1, SIDE):
+            shared.append(
+                pltpu.make_async_remote_copy(
+                    src_ref=held,
+                    dst_ref=held,
+                    send_sem=send_sems.at[step],
+                    recv_sem=recv_sems.at[step],
+                    device_id=(towards(step), m),
+                    device_id_type=MESH,
+                )
+            )
+        return shared
 
     add(cnt_local, 0, rows, feat, True)
 
-    pcopies = []
-    for dg in range(1, GROUPS):
-        pcopies.append(
-            pltpu.make_async_remote_copy(
-                src_ref=mine,
-                dst_ref=mine,
-                send_sem=pss.at[dg],
-                recv_sem=prs.at[dg],
-                device_id=(lax.rem(g + dg, GROUPS), m),
-                device_id_type=MESH,
-            )
-        )
-        pcopies[-1].start()
+    along_x = share(mine, beside, pss, prs)
+    for copy in along_x:
+        copy.start()
 
     def halo_place(b):
         t = b // 2
         dz = jnp.where(t == 0, 0, jnp.where(lax.rem(t, 2) == 1, 4 + t // 2, 4 - t // 2))
         j = lax.rem(z - dz + ZS, ZS) * 2 + lax.rem(c + lax.rem(b, 2), 2)
-        return lane + j * CAP
+        return column + j * CAP
 
     loads[3].wait()
-    counts(halon, 2, 2 * ZS, halo_place, cnt_halo)
-
-    for copy in pcopies:
+    counts(halon, 2, 0, ZS, halo_place, cnt_halo)
+
+    for copy in along_x:
+        copy.wait()
+    level = hubtab.at[pl.ds(pl.multiple_of(g // SIDE * SIDE * HUBZ, 16), SIDE * HUBZ), :]
+    along_y = share(level, above, yss, yrs)
+    for copy in along_y:
+        copy.start()
+
+    counts(halon, 2, ZS, 2 * ZS, halo_place, cnt_halo)
+
+    def inverse(i, carry):
+        at = pl.ds(pl.multiple_of(i * 128, 128), 128)
+        total = deg_ref[0:1, at] + deg_ref[1:2, at] + deg_ref[2:3, at]
+        inv[at, :] = 1.0 / jnp.maximum(spread(total).astype(F32), 1.0)
+        return carry
+
+    lax.fori_loop(0, rows // 128, inverse, 0)
+
+    def hub_place(b):
+        half = b // (HALF // 128)
+        p = column + 128 * lax.rem(b, HALF // 128)
+        group = p // HUBZ
+        inner = p - group * HUBZ
+        chip = inner // HUB
+        core = lax.rem(c + half, 2)
+        return ((group * ZS + chip) * 2 + core) * HUB + inner - chip * HUB
+
+    loads[4].wait()
+    counts(hubn, 1, 0, 2 * HALF // 128, hub_place, cnt_hub)
+
+    for copy in along_y:
         copy.wait()
     cross = pltpu.make_async_remote_copy(
         src_ref=hubtab.at[pl.ds(0, HALF), :],
@@ -270,26 +325,6 @@
         device_id_type=MESH,
     )
     cross.start()
-
-    def hub_place(b):
-        half = b // (HALF // 128)
-        p = lane + 128 * lax.rem(b, HALF // 128)
-        group = p // HUBZ
-        inner = p - group * HUBZ
-        chip = inner // HUB
-        core = lax.rem(c + half, 2)
-        return ((group * ZS + chip) * 2 + core) * HUB + inner - chip * HUB
-
-    loads[4].wait()
-    counts(hubn, 1, 2 * HALF // 128, hub_place, cnt_hub)
-
-    def inverse(i, carry):
-        at = pl.ds(pl.multiple_of(i * 128, 128), 128)
-        total = deg_ref[0:1, at] + deg_ref[1:2, at] + deg_ref[2:3, at]
-        inv[at, :] = 1.0 / jnp.maximum(spread(total).astype(F32), 1.0)
-        return carry
-
-    lax.fori_loop(0, rows // 128, inverse, 0)
 
     cross.wait()
     add(cnt_hub, 0, 2 * HALF, hubtab, False)
@@ -366,7 +401,7 @@
             pltpu.VMEM(halo_nbrs.shape[::-1], I32),
             pltpu.VMEM((2 * ZS * CAP, width), BF16),
             pltpu.VMEM((2 * ZS * CAP, width), BF16),
-            pltpu.VMEM((ZS, HUBP, width), BF16),
+            pltpu.VMEM((ZS, HUBZ, 128), BF16),
             pltpu.VMEM((2 * HALF, width), BF16),
             pltpu.VMEM((rows, rows), BF16),
             pltpu.VMEM((rows, 2 * HALF), BF16),
@@ -381,8 +416,10 @@
             dma((2, 16)),
             dma((ZS,)),
             dma((ZS,)),
-            dma((GROUPS,)),
-            dma((GROUPS,)),
+            dma((SIDE,)),
+            dma((SIDE,)),
+            dma((SIDE,)),
+            dma((SIDE,)),
             dma,
             dma,
         ],

time: 113 us -> 110 us (0.973)
  Pallas kernels: 111 us -> 109 us
    pallas_call x1, Pallas kernels: 111 us -> 109 us  [per_device(): pl.pallas_call(kernel, out_shape=pltpu.VMEM((rows, wide_out), BF16), in_s...]
where the time goes in v3:
time: 110 us
  Pallas kernels  109 us (99%)
  local copies, waits for them, and re-layouts  1.32 us (1%)
    pallas_call x1, Pallas kernels, per_device(): pl.pallas_call(kernel, out_shape=pltpu.VMEM((rows, wide_out), BF16), in_s...  109 us

profile of v3, /device:TPU:1, one launch (start us, length us, event | category | flops | bytes accessed | tf_op | source)
XLA Modules:
  0.0 110.1 jit_solution(14960733892702653295)
XLA Ops:
  0.0 108.7 %shard_map.100 = bf16[1024,1024]{1,0:T(8,128)(2,1)S(1)} custom-call(s32[6]{0:T(128)} %hub_rows.1, bf16[1024,1024]{1,0:T(8,128)(2,1)} %feat_hbm.1, bf16[1024,1024]{1,0:T(8,128)(2,1)} %ws_hbm.1, bf16[1024,1024]{1,0:T(8,128)(2,1)} %wn_hbm.1, bf16[1024]{0:T(1024)(128)(2,1)} %bias_ref.1, s32[8,1024]{1,0:T(8,128)} %bitcast.5, s32[16,1024]{1,0:T(8,128)} %bitcast.3, ...), custom_call_target="tpu_custom_call" | custom-call | tf_op jit(solution)/shard_map/pallas_call | solution.py:379
  108.7 1.3 %copy.12 = bf16[1024,1024]{1,0:T(8,128)(2,1)} copy(bf16[1024,1024]{1,0:T(8,128)(2,1)S(1)} %shard_map.100) | data formatting | bytes 4194304

commit v4 on v3

--- a/solution.py
+++ b/solution.py
@@ -19,6 +19,9 @@
 HUBZ = ZS * HUB
 HALF = GROUPS * HUBZ
 CHUNK = 256
+MORE = 512
+LAST = 512
+BOUNDS = (0, 512, 1024)
 STEPS = (0, 4, 3, 5, 2, 6, 1, 7)
 
 
@@ -81,7 +84,7 @@
     z = m // 2
     c = lax.rem(m, 2)
     rows = feat.shape[0]
-    split = feat.shape[1] * 3 // 4
+    parts = [pl.ds(a, b - a) for a, b in zip(BOUNDS, BOUNDS[1:])]
 
     def peer(dz, dc):
         return lax.rem(z + dz, ZS) * 2 + lax.rem(c + dc, 2)
@@ -133,17 +136,17 @@
     hubz[0] = packed.astype(BF16)
 
     def pick(t):
-        parts = []
+        hots = []
         for dc in range(2):
             row = spread(send_ref[0, pl.ds(peer(STEPS[t], dc), 1), :])
-            parts.append(
+            hots.append(
                 jnp.concatenate(
                     [jnp.where(row == lane + 128 * b, 1.0, 0.0).astype(BF16) for b in range(rows // 128)],
                     axis=1,
                 )
             )
         at = pl.ds(2 * t * CAP, 2 * CAP)
-        sendbuf[at, :] = dot(jnp.concatenate(parts, axis=0), feat[...]).astype(BF16)
+        sendbuf[at, :] = dot(jnp.concatenate(hots, axis=0), feat[...]).astype(BF16)
 
     for t in range(1, 5):
         pick(t)
@@ -178,7 +181,6 @@
         copies[t, dc, part] = copy
         copy.start()
 
-    head, tail = pl.ds(0, split), pl.ds(split, feat.shape[1] - split)
     both = pl.ds(0, feat.shape[1])
     for t in (1, 2):
         send(t, 0, 0, both)
@@ -190,7 +192,7 @@
         send(t, 1, 0, both)
     pick(7)
     pick(0)
-    for part, columns in enumerate((head, tail)):
+    for part, columns in enumerate(parts):
         for t in (6, 7):
             send(t, 0, part, columns)
             send(t, 1, part, columns)
@@ -339,33 +341,26 @@
 
     loads[5].wait()
 
-    def last_blocks(i, columns):
-        at = pl.ds(pl.multiple_of(i * CHUNK, CHUNK), CHUNK)
-        total = acc[at, columns] + dot(cnt_halo[at, 12 * CAP :], recv[12 * CAP :, columns])
-        mean = total * jnp.concatenate([inv[at, :]] * (total.shape[1] // 128), axis=1)
-        return at, own[at, :] + dot(mean.astype(BF16), wn[columns, :])
-
-    for t in (6, 7):
-        copies[t, 0, 0].wait()
-        copies[t, 1, 0].wait()
-
-    def first_columns(i, carry):
-        at, value = last_blocks(i, head)
-        own[at, :] = value
-        return carry
-
-    lax.fori_loop(0, rows // CHUNK, first_columns, 0)
-
-    for t in (6, 7):
-        copies[t, 0, 1].wait()
-        copies[t, 1, 1].wait()
-
-    def last_columns(i, carry):
-        at, value = last_blocks(i, tail)
-        out_ref[at, :] = jnp.maximum(value, 0.0).astype(BF16)
-        return carry
-
-    lax.fori_loop(0, rows // CHUNK, last_columns, 0)
+    def last_blocks(columns, size, finish):
+        def some_rows(i, carry):
+            at = pl.ds(pl.multiple_of(i * size, size), size)
+            total = acc[at, columns] + dot(cnt_halo[at, 12 * CAP :], recv[12 * CAP :, columns])
+            mean = total * jnp.concatenate([inv[at, :]] * (total.shape[1] // 128), axis=1)
+            value = own[at, :] + dot(mean.astype(BF16), wn[columns, :])
+            if finish:
+                out_ref[at, :] = jnp.maximum(value, 0.0).astype(BF16)
+            else:
+                own[at, :] = value
+            return carry
+
+        lax.fori_loop(0, rows // size, some_rows, 0)
+
+    for part, columns in enumerate(parts):
+        for t in (6, 7):
+            copies[t, 0, part].wait()
+            copies[t, 1, part].wait()
+        finish = part == len(parts) - 1
+        last_blocks(columns, LAST if finish else MORE, finish)
 
 
 def per_device(
@@ -412,8 +407,8 @@
             pltpu.VMEM((rows, wide_out), F32),
             dma((6,)),
             dma,
-            dma((2, 16)),
-            dma((2, 16)),
+            dma((len(BOUNDS) - 1, 16)),
+            dma((len(BOUNDS) - 1, 16)),
             dma((ZS,)),
             dma((ZS,)),
             dma((SIDE,)),

time: 110 us -> 109 us (level)
  Pallas kernels: 109 us -> 107 us
    pallas_call x1, Pallas kernels: 109 us -> 107 us  [per_device(): pl.pallas_call(kernel, out_shape=pltpu.VMEM((rows, wide_out), BF16), in_s...]
where the time goes in v4:
time: 109 us
  Pallas kernels  107 us (98%)
  local copies, waits for them, and re-layouts  1.32 us (1%)
    pallas_call x1, Pallas kernels, per_device(): pl.pallas_call(kernel, out_shape=pltpu.VMEM((rows, wide_out), BF16), in_s...  107 us

profile of v4, /device:TPU:1, one launch (start us, length us, event | category | flops | bytes accessed | tf_op | source)
XLA Modules:
  0.0 108.8 jit_solution(18082279588301654726)
XLA Ops:
  0.0 107.4 %shard_map.100 = bf16[1024,1024]{1,0:T(8,128)(2,1)S(1)} custom-call(s32[6]{0:T(128)} %hub_rows.1, bf16[1024,1024]{1,0:T(8,128)(2,1)} %feat_hbm.1, bf16[1024,1024]{1,0:T(8,128)(2,1)} %ws_hbm.1, bf16[1024,1024]{1,0:T(8,128)(2,1)} %wn_hbm.1, bf16[1024]{0:T(1024)(128)(2,1)} %bias_ref.1, s32[8,1024]{1,0:T(8,128)} %bitcast.5, s32[16,1024]{1,0:T(8,128)} %bitcast.3, ...), custom_call_target="tpu_custom_call" | custom-call | tf_op jit(solution)/shard_map/pallas_call | solution.py:374
  107.4 1.3 %copy.12 = bf16[1024,1024]{1,0:T(8,128)(2,1)} copy(bf16[1024,1024]{1,0:T(8,128)(2,1)S(1)} %shard_map.100) | data formatting | bytes 4194304

commit v5 on v4

--- a/solution.py
+++ b/solution.py
@@ -21,7 +21,7 @@
 CHUNK = 256
 MORE = 512
 LAST = 512
-BOUNDS = (0, 512, 1024)
+BOUNDS = (0, 640, 1024)
 STEPS = (0, 4, 3, 5, 2, 6, 1, 7)
 
 

time: 109 us -> 109 us (level)
  no operation moved by 1% of the time
where the time goes in v5:
time: 109 us
  Pallas kernels  107 us (98%)
  local copies, waits for them, and re-layouts  1.32 us (1%)
    pallas_call x1, Pallas kernels, per_device(): pl.pallas_call(kernel, out_shape=pltpu.VMEM((rows, wide_out), BF16), in_s...  107 us

profile of v5, /device:TPU:1, one launch (start us, length us, event | category | flops | bytes accessed | tf_op | source)
XLA Modules:
  0.0 108.8 jit_solution(10698568284168996494)
XLA Ops:
  0.0 107.4 %shard_map.100 = bf16[1024,1024]{1,0:T(8,128)(2,1)S(1)} custom-call(s32[6]{0:T(128)} %hub_rows.1, bf16[1024,1024]{1,0:T(8,128)(2,1)} %feat_hbm.1, bf16[1024,1024]{1,0:T(8,128)(2,1)} %ws_hbm.1, bf16[1024,1024]{1,0:T(8,128)(2,1)} %wn_hbm.1, bf16[1024]{0:T(1024)(128)(2,1)} %bias_ref.1, s32[8,1024]{1,0:T(8,128)} %bitcast.5, s32[16,1024]{1,0:T(8,128)} %bitcast.3, ...), custom_call_target="tpu_custom_call" | custom-call | tf_op jit(solution)/shard_map/pallas_call | solution.py:374
  107.4 1.3 %copy.12 = bf16[1024,1024]{1,0:T(8,128)(2,1)} copy(bf16[1024,1024]{1,0:T(8,128)(2,1)S(1)} %shard_map.100) | data formatting | bytes 4194304
